TPU v7x, 32 devices: a whole 2x2x4 slice. The times are simulated.
32 devices in a mesh: grp: 2 (over x), exp: 16 (over z, y, core).
Axes of the slice: x: 2, y: 2, z: 4, core: 2. Of those that a mesh axis runs over, the one named last changes fastest.
Arguments:
- hidden: bfloat16 [32, 4096], P(('grp', 'exp')), may hold values from -6 to 6
- route_ids: int32 [32, 8], P(('grp', 'exp')), may hold values from 0 to 15, all different within a row; in each aligned block of 32 rows (0 to 31, 32 to 63, ...) at most 32 rows name the same one
- route_logits: bfloat16 [32, 8], P(('grp', 'exp')), may hold values from -6 to 6
- sampled: int32 [32], P(('grp', 'exp')), may hold values from 0 to 131071
- norm_gain: float32 [4096], replicated, may hold values from 0.5 to 1.5
- gate_weight: bfloat16 [16, 4096, 1536], P('exp', 'grp'), may hold values from -0.09375 to 0.09375
- up_weight: bfloat16 [16, 4096, 1536], P('exp', 'grp'), may hold values from -0.09375 to 0.09375
- down_weight: bfloat16 [16, 1536, 4096], P('exp', None, 'grp'), may hold values from -0.15625 to 0.15625
- head_weight: bfloat16 [4096, 131072], P(None, ('grp', 'exp')), may hold values from -0.25 to 0.25
- noise_steps: int32 [131072], P(('grp', 'exp')), may hold values from -64 to 64
Outputs:
- vote_counts: float32 [131072], P(('grp', 'exp'))
- log_ratio: float32 [32], P(('grp', 'exp'))
Inputs may be any that keep to these rules, and one draw needn't show every extreme that they name: `route_ids`: each row names 8 different experts. Over all 32 rows no expert is named by more than 32 rows, a bound that some block reaches.
All inputs are finite; a program needn't handle non-finite values.
Results may differ from a plain program's by a relative error of at most 0.004.
Values may be sent and summed in bfloat16 or wider, within the bound.
A program may use at most 128 MiB of HBM per device.

v0:
```python
import jax
import jax.numpy as jnp
from jax import lax
from jax.sharding import PartitionSpec as P

TOPK = 8
VOCAB = 131072
clip_bound = 8.0
noise_step = 0.03125
norm_eps = 1e-06


def on_device(
    hidden,
    route_ids,
    route_logits,
    sampled,
    norm_gain,
    gate_weight,
    up_weight,
    down_weight,
    head_weight,
    noise_steps,
):
    groups = lax.axis_size("grp")
    columns_count = lax.axis_size("exp")
    width = gate_weight.shape[1]
    column_index = lax.axis_index("exp")
    device_index = lax.axis_index(("grp", "exp"))
    group_rows, group_ids, group_logits, group_sampled = (
        lax.all_gather(hidden, "exp", axis=0, tiled=True),
        lax.all_gather(route_ids, "exp", axis=0, tiled=True),
        lax.all_gather(route_logits, "exp", axis=0, tiled=True),
        lax.all_gather(sampled, "exp", axis=0, tiled=True),
    )
    row_count = group_rows.shape[0]
    topk_width = group_ids.shape[1]
    pieces = group_rows.reshape(row_count, groups, width)
    ids_spread = jnp.broadcast_to(group_ids[:, None, :], (row_count, groups, topk_width))
    logits_spread = jnp.broadcast_to(group_logits[:, None, :], (row_count, groups, topk_width))
    sampled_spread = jnp.broadcast_to(group_sampled[:, None, None], (row_count, groups, 1))
    arrived = (
        lax.all_to_all(pieces, "grp", split_axis=1, concat_axis=0, tiled=True),
        lax.all_to_all(ids_spread, "grp", split_axis=1, concat_axis=0, tiled=True),
        lax.all_to_all(logits_spread, "grp", split_axis=1, concat_axis=0, tiled=True),
        lax.all_to_all(sampled_spread, "grp", split_axis=1, concat_axis=0, tiled=True),
    )
    member_count = row_count * groups
    width_slab = arrived[0].reshape(member_count, width)
    ids_all = arrived[1].reshape(member_count, topk_width)
    logits_all = arrived[2].reshape(member_count, topk_width)
    sampled_all = arrived[3].reshape(member_count)
    members_total = width_slab.shape[0]
    capacity = min(members_total, 2 * members_total * TOPK // columns_count)
    mixing = jax.nn.softmax(logits_all.astype(jnp.float32), axis=-1)
    matches = ids_all == column_index
    chosen = jnp.any(matches, axis=1)
    share = jnp.sum(jnp.where(matches, mixing, 0.0), axis=1)
    position = jnp.cumsum(chosen.astype(jnp.int32)) - 1
    slot_index = jnp.arange(capacity, dtype=jnp.int32)
    select = ((position[None, :] == slot_index[:, None]) & chosen[None, :]).astype(jnp.bfloat16)
    picked = jnp.dot(select, width_slab, preferred_element_type=jnp.float32).astype(jnp.bfloat16)
    gate_part = jnp.dot(picked, gate_weight[0], preferred_element_type=jnp.float32)
    upward_part = jnp.dot(picked, up_weight[0], preferred_element_type=jnp.float32)
    gate_sum, upward_sum = lax.psum((gate_part, upward_part), "grp")
    active = (jax.nn.silu(gate_sum) * upward_sum).astype(jnp.bfloat16)
    output = jnp.dot(active, down_weight[0], preferred_element_type=jnp.float32).astype(
        jnp.bfloat16
    )
    spread = jnp.einsum("cm,cw->mw", select, output, preferred_element_type=jnp.float32)
    contrib = spread * share[:, None]
    moe_slab = lax.psum(contrib, "exp")
    residual = (width_slab.astype(jnp.float32) + moe_slab).astype(jnp.bfloat16)
    vocab_block = head_weight.shape[1]
    piece = lax.all_gather(residual, "grp", axis=1, tiled=True)
    scaled = (piece.astype(jnp.float32) * norm_gain[None, :]).astype(jnp.bfloat16)
    acc_logits = jnp.dot(scaled, head_weight, preferred_element_type=jnp.float32)
    acc_squares = jnp.sum(jnp.square(piece.astype(jnp.float32)), axis=1)
    model_width = norm_gain.shape[0]
    root_mean = jnp.sqrt(acc_squares / model_width + norm_eps)
    logits = acc_logits / root_mean[:, None]
    clipped = jnp.clip(logits, -clip_bound, clip_bound)
    exp_values = jnp.exp(clipped)
    first_column = device_index * vocab_block
    vocab_columns = first_column + jnp.arange(vocab_block, dtype=jnp.int32)
    owned = sampled_all[:, None] == vocab_columns[None, :]
    part_total = jnp.sum(exp_values, axis=1)
    part_chosen = jnp.sum(jnp.where(owned, clipped, 0.0), axis=1)
    totals, chosen_logit = lax.psum((part_total, part_chosen), ("grp", "exp"))
    log_ratio = chosen_logit - jnp.log(totals / VOCAB)
    own_rows = hidden.shape[0]
    own_ratio = lax.dynamic_slice_in_dim(log_ratio, device_index * own_rows, own_rows, 0)
    vote_counts = (
        VOCAB / members_total * jnp.sum(exp_values / totals[:, None], axis=0)
        + noise_steps.astype(jnp.float32) * noise_step
    )
    return (vote_counts, own_ratio)


def solution(mesh):
    placed = (
        P(("grp", "exp"), None),
        P(("grp", "exp"), None),
        P(("grp", "exp"), None),
        P(("grp", "exp")),
        P(),
        P("exp", "grp", None),
        P("exp", "grp", None),
        P("exp", None, "grp"),
        P(None, ("grp", "exp")),
        P(("grp", "exp")),
    )
    return jax.shard_map(
        on_device,
        mesh=mesh,
        in_specs=placed,
        out_specs=(P(("grp", "exp")), P(("grp", "exp"))),
        check_vma=False,
    )
```

profile of v0, /device:TPU:0, one launch (start us, length us, event | category | flops | bytes accessed | tf_op | source)
XLA Modules:
  0.0 297.2 jit_solution(6315251923228911917)
XLA Ops:
  7.2 23.3 %all-gather.1 = s32[16,1,8]{2,1,0:T(1,128)S(1)} all-gather(s32[1,1,8]{2,1,0:T(1,128)} %bitcast.59), channel_id=1, replica_groups=mesh['grp'=2,'exp'=16] {'exp'}, dimensions={0}, use_global_device_ids=true | all-gather | bytes 544 | tf_op jit(solution)/shard_map/all_gather | solution.py:32
  30.5 0.6 reshape.123
  31.2 3.2 %all-to-all-start.1 = ((s32[2,1,128]{2,1,0:T(1,128)}), s32[2,1,128]{2,1,0:T(1,128)S(1)}, u32[]{:S(2)}, u32[]{:S(2)}) async-start(s32[2,1,128]{2,1,0:T(1,128)} %reshape.123), calls=%async_computation.1 | async-start | bytes 2048 | tf_op jit(solution)/shard_map/all_to_all | solution.py:44
  34.4 18.4 %all-gather = bf16[16,1,4096]{2,1,0:T(2,128)(2,1)S(1)} all-gather(bf16[1,1,4096]{2,1,0:T(2,128)(2,1)} %bitcast.55), channel_id=1, replica_groups=mesh['grp'=2,'exp'=16] {'exp'}, dimensions={0}, use_global_device_ids=true | all-gather | bytes 139264 | tf_op jit(solution)/shard_map/all_gather | solution.py:31
  52.8 0.7 reduce.5
  53.5 0.6 copy.29
  54.2 3.4 %all-to-all-start = ((bf16[16,2,2048]{2,0,1:T(8,128)(2,1)}), bf16[16,2,2048]{2,0,1:T(8,128)(2,1)S(1)}, u32[]{:S(2)}, u32[]{:S(2)}) async-start(bf16[16,2,2048]{2,0,1:T(8,128)(2,1)} %bitcast.52), calls=%async_computation | async-start | bytes 262144 | tf_op jit(solution)/shard_map/all_to_all | solution.py:43
  58.1 0.7 reduce.8
  59.2 2.9 all-to-all-done
  62.3 4.8 %fusion.2 = f32[32,1536]{1,0:T(8,128)} fusion(bf16[32,2048]{1,0:T(8,128)(2,1)S(1)} %convolution_convert_fusion, bf16[1,2048,1536]{2,1,0:T(8,128)(2,1)} %param.16), kind=kOutput, calls=%fused_computation.2 | convolution fusion | flops 201326592 | bytes 6619136 | tf_op jit(solution)/shard_map/dot_general | solution.py:64
  67.0 1.8 fusion.4
  68.9 19.2 %all-gather.2 = bf16[16,1,8]{2,1,0:T(2,128)(2,1)S(1)} all-gather(bf16[1,1,8]{2,1,0:T(2,128)(2,1)S(1)} %bitcast.60), channel_id=1, replica_groups=mesh['grp'=2,'exp'=16] {'exp'}, dimensions={0}, use_global_device_ids=true | all-gather | bytes 272 | tf_op jit(solution)/shard_map/all_gather | solution.py:33
  88.2 6.1 %all_to_all.54 = bf16[16,2,8]{0,2,1:T(8,128)(2,1)S(1)} all-to-all(bf16[16,2,8]{0,2,1:T(8,128)(2,1)S(1)} %broadcast_in_dim.13), channel_id=1, replica_groups=mesh['grp'=2,'exp'=16] {'grp'}, dimensions={1} | all-to-all | bytes 1024 | tf_op jit(solution)/shard_map/all_to_all | solution.py:45
  94.5 5.0 %convolution_multiply_fusion = f32[32,2048]{1,0:T(8,128)} fusion(bf16[1,1536,2048]{2,1,0:T(8,128)(2,1)} %param.17, f32[32]{0:T(128)S(1)} %mul.45, f32[32,1536]{1,0:T(8,128)} %get-tuple-element.4, f32[32,1536]{1,0:T(8,128)} %get-tuple-element.5, s32[32]{0:T(128)S(1)} %add_reduce_fusion, pred[32]{0:T(512)(128)(4,1)S(1)} %and.12), kind=kOutput, calls=%fused_computation.8 | convolution fusion | flops 205948928 | bytes 6947104 | tf_op jit(solution)/shard_map/cm,cw->mw/dot_general | solution.py:70
  100.8 0.8 dynamic-update-slice
  101.5 10.2 %all-reduce = s32[16]{0:T(128)S(1)} all-reduce(s32[16]{0:T(128)S(1)} %dynamic-update-slice), channel_id=1, replica_groups=mesh['grp'=2,'exp'=16] {'exp'}, use_global_device_ids=true, to_apply=%add | all-reduce | flops 16 | bytes 128
  112.3 3.2 %all-to-all-start.3 = ((s32[16,2,1]{0,2,1:T(1,128)}), s32[16,2,1]{0,2,1:T(1,128)S(1)}, u32[]{:S(2)}, u32[]{:S(2)}) async-start(s32[16,2,1]{0,2,1:T(1,128)} %broadcast_in_dim.16), calls=%async_computation.3 | async-start | bytes 2048 | tf_op jit(solution)/shard_map/all_to_all | solution.py:46
  115.5 3.7 %all-to-all-done.3 = s32[16,2,1]{0,2,1:T(1,128)S(1)} async-done(((s32[16,2,1]{0,2,1:T(1,128)}), s32[16,2,1]{0,2,1:T(1,128)S(1)}, u32[]{:S(2)}, u32[]{:S(2)}) %all-to-all-start.3) | async-done | bytes 160 | tf_op jit(solution)/shard_map/all_to_all | solution.py:46
  119.3 68.5 %all-reduce.5.cloned.1.call-done = f32[32,2048]{1,0:T(8,128)} async-done(((f32[32,2048]{1,0:T(8,128)}), f32[32,2048]{1,0:T(8,128)}) %all-reduce.5.cloned.1.call-update) | async-done | bytes 262160 | tf_op jit(solution)/shard_map/psum | solution.py:72
  187.8 1.0 add_convert_fusion
  188.8 6.5 %all_gather.18 = bf16[32,4096]{1,0:T(8,128)(2,1)S(1)} all-gather(bf16[32,2048]{1,0:T(8,128)(2,1)S(1)} %add_convert_fusion), channel_id=1, replica_groups=mesh['grp'=2,'exp'=16] {'grp'}, dimensions={1}, use_global_device_ids=true | all-gather | bytes 393216 | tf_op jit(solution)/shard_map/all_gather | solution.py:75
  195.5 13.7 %exponential_reduce_fusion = (f32[32]{0:T(128)S(1)}, f32[32,4096]{1,0:T(8,128)S(1)}) fusion(f32[32]{0:T(128)S(1)} %add_sqrt_fusion, bf16[4096,4096]{1,0:T(8,128)(2,1)} %param.18, bf16[32,4096]{1,0:T(8,128)(2,1)S(1)} %all_gather.18, f32[4096]{0:T(1024)S(1)} %copy-done.1), kind=kOutput, calls=%fused_computation.17 | convolution fusion | flops 1074528256 | bytes 34357504 | tf_op jit(solution)/shard_map/dot_general | solution.py:77
  209.2 39.8 %psum.38 = f32[32]{0:T(128)S(1)} all-reduce(f32[32]{0:T(128)S(1)} %get-tuple-element.8), channel_id=1, replica_groups=mesh['grp'=2,'exp'=16] {'grp','exp'}, use_global_device_ids=true, to_apply=%region_10.11 | all-reduce | flops 32 | bytes 256 | tf_op jit(solution)/shard_map/psum | solution.py:89
  249.2 39.9 %psum.39 = f32[32]{0:T(128)S(1)} all-reduce(f32[32]{0:T(128)S(1)} %get-tuple-element.2), channel_id=1, replica_groups=mesh['grp'=2,'exp'=16] {'grp','exp'}, use_global_device_ids=true, to_apply=%region_13.14 | all-reduce | flops 32 | bytes 256 | tf_op jit(solution)/shard_map/psum | solution.py:89
  (45 shorter events, 4.5 us)
Async XLA Ops:
  31.2 23.0 %all-to-all-start.1 = ((s32[2,1,128]{2,1,0:T(1,128)}), s32[2,1,128]{2,1,0:T(1,128)S(1)}, u32[]{:S(2)}, u32[]{:S(2)}) async-start(s32[2,1,128]{2,1,0:T(1,128)} %reshape.123), calls=%async_computation.1 | async-start | bytes 2048 | tf_op jit(solution)/shard_map/all_to_all | solution.py:44
  54.2 7.9 %all-to-all-start = ((bf16[16,2,2048]{2,0,1:T(8,128)(2,1)}), bf16[16,2,2048]{2,0,1:T(8,128)(2,1)S(1)}, u32[]{:S(2)}, u32[]{:S(2)}) async-start(bf16[16,2,2048]{2,0,1:T(8,128)(2,1)} %bitcast.52), calls=%async_computation | async-start | bytes 262144 | tf_op jit(solution)/shard_map/all_to_all | solution.py:43
  57.6 36.9 %all-reduce.7.cloned.1.call-start = ((), (), s32[]{:S(2)}) async-start(), calls=%async_computation.5 | async-start | bytes 786432 | tf_op jit(solution)/shard_map/psum | solution.py:65
  62.1 4.9 %copy-start = (bf16[1,2048,1536]{2,1,0:T(8,128)(2,1)S(1)}, bf16[1,2048,1536]{2,1,0:T(8,128)(2,1)}, u32[]{:S(2)}) copy-start(bf16[1,2048,1536]{2,1,0:T(8,128)(2,1)} %param.15) | copy-start | bytes 18874372
  62.3 6.7 %copy-start.3 = (bf16[1,8]{1,0:T(2,128)(2,1)S(1)}, bf16[1,8]{1,0:T(2,128)(2,1)}, u32[]{:S(2)}) copy-start(bf16[1,8]{1,0:T(2,128)(2,1)} %param.12) | copy-start | bytes 52
  67.0 33.1 %copy-start.4 = (u32[32]{0:T(128)S(1)}, u32[32]{0:T(128)}, u32[]{:S(2)}) copy-start(u32[32]{0:T(128)} %constant.59) | copy-start | bytes 388
  67.0 128.4 %copy-start.1 = (f32[4096]{0:T(1024)S(1)}, f32[4096]{0:T(1024)}, u32[]{:S(2)}) copy-start(f32[4096]{0:T(1024)} %param.14) | copy-start | bytes 49156
  68.9 118.9 %all-reduce.5.cloned.1.call-start = ((), (), s32[]{:S(2)}) async-start(), calls=%async_computation.4 | async-start | bytes 524288 | tf_op jit(solution)/shard_map/psum | solution.py:72
  112.3 6.9 %all-to-all-start.3 = ((s32[16,2,1]{0,2,1:T(1,128)}), s32[16,2,1]{0,2,1:T(1,128)S(1)}, u32[]{:S(2)}, u32[]{:S(2)}) async-start(s32[16,2,1]{0,2,1:T(1,128)} %broadcast_in_dim.16), calls=%async_computation.3 | async-start | bytes 2048 | tf_op jit(solution)/shard_map/all_to_all | solution.py:46
  195.5 93.7 %copy-start.2 = (s32[4096]{0:T(1024)S(1)}, s32[4096]{0:T(1024)}, u32[]{:S(2)}) copy-start(s32[4096]{0:T(1024)} %param.19) | copy-start | bytes 49156
Sparse Core Ops, SparseCore 0:
  69.0 23.5 all-reduce.6
  99.6 88.1 all-reduce.4
where the time goes:
time: 298 us; the launch traced here: 297 us
  blocking collectives  163 us (55%)
  waiting for transfers between devices  75.1 us (25%)
  matrix products  25.4 us (9%)
  between operations  14.8 us (5%)
  starting transfers between devices  9.85 us (3%)
  local copies, waits for them, and re-layouts  4.89 us (2%)
  other arithmetic  3.71 us (1%)
    psum x2, blocking collectives, on_device(): totals, chosen_logit = lax.psum((part_total, part_chosen), ('grp', 'exp'))  79.7 us
    psum x1, waiting for transfers between devices, on_device(): moe_slab = lax.psum(contrib, 'exp')  68.5 us
    all_gather x1, blocking collectives, on_device(): lax.all_gather(route_ids, 'exp', axis=0, tiled=True)  23.3 us
    all_gather x1, blocking collectives, on_device(): lax.all_gather(route_logits, 'exp', axis=0, tiled=True)  19.2 us
    all_gather x1, blocking collectives, on_device(): lax.all_gather(hidden, 'exp', axis=0, tiled=True)  18.4 us
    dot_general x1, matrix products, on_device(): jnp.dot(scaled, head_weight, preferred_element_type=jnp.float32)  13.7 us
    unnamed x1, blocking collectives  10.2 us
    all_gather x1, blocking collectives, on_device(): piece = lax.all_gather(residual, 'grp', axis=1, tiled=True)  6.51 us
  transfers between devices with their start and end apart: 5, of which 3 were waited for; matrix products, arithmetic and copies ran while one was open for 2% of the time, Pallas kernels for 0%

commit v1 on v0

--- a/solution.py
+++ b/solution.py
@@ -86,7 +86,7 @@
     owned = sampled_all[:, None] == vocab_columns[None, :]
     part_total = jnp.sum(exp_values, axis=1)
     part_chosen = jnp.sum(jnp.where(owned, clipped, 0.0), axis=1)
-    totals, chosen_logit = lax.psum((part_total, part_chosen), ("grp", "exp"))
+    totals, chosen_logit = jax.lax.psum(jax.lax.psum((part_total, part_chosen), "grp"), "exp")
     log_ratio = chosen_logit - jnp.log(totals / VOCAB)
     own_rows = hidden.shape[0]
     own_ratio = lax.dynamic_slice_in_dim(log_ratio, device_index * own_rows, own_rows, 0)

time: 298 us -> 287 us (0.963)
  blocking collectives: 163 us -> 152 us
    psum x2 -> x4, blocking collectives: 79.7 us -> 68.8 us  [the longest x2 58.9 us: on_device(): jax.lax.psum(jax.lax.psum((part_total, part_chosen), 'grp'), 'exp')]
where the time goes in v1:
time: 287 us; the launch traced here: 286 us
  blocking collectives  152 us (53%)
  waiting for transfers between devices  75.1 us (26%)
  matrix products  25.4 us (9%)
  between operations  14.8 us (5%)
  starting transfers between devices  9.85 us (3%)
  local copies, waits for them, and re-layouts  4.89 us (2%)
  other arithmetic  3.71 us (1%)
    psum x1, waiting for transfers between devices, on_device(): moe_slab = lax.psum(contrib, 'exp')  68.5 us
    psum x2, blocking collectives, on_device(): jax.lax.psum(jax.lax.psum((part_total, part_chosen), 'grp'), 'exp')  58.9 us
    all_gather x1, blocking collectives, on_device(): lax.all_gather(route_ids, 'exp', axis=0, tiled=True)  23.3 us
    all_gather x1, blocking collectives, on_device(): lax.all_gather(route_logits, 'exp', axis=0, tiled=True)  19.2 us
    all_gather x1, blocking collectives, on_device(): lax.all_gather(hidden, 'exp', axis=0, tiled=True)  18.4 us
    dot_general x1, matrix products, on_device(): jnp.dot(scaled, head_weight, preferred_element_type=jnp.float32)  13.7 us
    unnamed x1, blocking collectives  10.2 us
    psum x2, blocking collectives, on_device(): jax.lax.psum((part_total, part_chosen), 'grp')  9.86 us
  transfers between devices with their start and end apart: 5, of which 3 were waited for; matrix products, arithmetic and copies ran while one was open for 2% of the time, Pallas kernels for 0%

profile of v1, /device:TPU:0, one launch (start us, length us, event | category | flops | bytes accessed | tf_op | source)
XLA Modules:
  0.0 286.3 jit_solution(1715758485845592837)
XLA Ops:
  7.2 23.3 %all-gather.1 = s32[16,1,8]{2,1,0:T(1,128)S(1)} all-gather(s32[1,1,8]{2,1,0:T(1,128)} %bitcast.59), channel_id=1, replica_groups=mesh['grp'=2,'exp'=16] {'exp'}, dimensions={0}, use_global_device_ids=true | all-gather | bytes 544 | tf_op jit(solution)/shard_map/all_gather | solution.py:32
  31.2 3.2 %all-to-all-start.1 = ((s32[2,1,128]{2,1,0:T(1,128)}), s32[2,1,128]{2,1,0:T(1,128)S(1)}, u32[]{:S(2)}, u32[]{:S(2)}) async-start(s32[2,1,128]{2,1,0:T(1,128)} %reshape.123), calls=%async_computation.1 | async-start | bytes 2048 | tf_op jit(solution)/shard_map/all_to_all | solution.py:44
  34.4 18.4 %all-gather = bf16[16,1,4096]{2,1,0:T(2,128)(2,1)S(1)} all-gather(bf16[1,1,4096]{2,1,0:T(2,128)(2,1)} %bitcast.55), channel_id=1, replica_groups=mesh['grp'=2,'exp'=16] {'exp'}, dimensions={0}, use_global_device_ids=true | all-gather | bytes 139264 | tf_op jit(solution)/shard_map/all_gather | solution.py:31
  52.8 0.7 reduce.5
  54.2 3.4 %all-to-all-start = ((bf16[16,2,2048]{2,0,1:T(8,128)(2,1)}), bf16[16,2,2048]{2,0,1:T(8,128)(2,1)S(1)}, u32[]{:S(2)}, u32[]{:S(2)}) async-start(bf16[16,2,2048]{2,0,1:T(8,128)(2,1)} %bitcast.52), calls=%async_computation | async-start | bytes 262144 | tf_op jit(solution)/shard_map/all_to_all | solution.py:43
  58.1 0.7 reduce.8
  59.2 2.9 all-to-all-done
  62.3 4.8 %fusion.2 = f32[32,1536]{1,0:T(8,128)} fusion(bf16[32,2048]{1,0:T(8,128)(2,1)S(1)} %convolution_convert_fusion, bf16[1,2048,1536]{2,1,0:T(8,128)(2,1)} %param.16), kind=kOutput, calls=%fused_computation.2 | convolution fusion | flops 201326592 | bytes 6619136 | tf_op jit(solution)/shard_map/dot_general | solution.py:64
  67.0 1.8 fusion.4
  68.9 19.2 %all-gather.2 = bf16[16,1,8]{2,1,0:T(2,128)(2,1)S(1)} all-gather(bf16[1,1,8]{2,1,0:T(2,128)(2,1)S(1)} %bitcast.60), channel_id=1, replica_groups=mesh['grp'=2,'exp'=16] {'exp'}, dimensions={0}, use_global_device_ids=true | all-gather | bytes 272 | tf_op jit(solution)/shard_map/all_gather | solution.py:33
  88.2 6.1 %all_to_all.54 = bf16[16,2,8]{0,2,1:T(8,128)(2,1)S(1)} all-to-all(bf16[16,2,8]{0,2,1:T(8,128)(2,1)S(1)} %broadcast_in_dim.13), channel_id=1, replica_groups=mesh['grp'=2,'exp'=16] {'grp'}, dimensions={1} | all-to-all | bytes 1024 | tf_op jit(solution)/shard_map/all_to_all | solution.py:45
  94.5 5.0 %convolution_multiply_fusion = f32[32,2048]{1,0:T(8,128)} fusion(bf16[1,1536,2048]{2,1,0:T(8,128)(2,1)} %param.17, f32[32]{0:T(128)S(1)} %mul.45, f32[32,1536]{1,0:T(8,128)} %get-tuple-element.4, f32[32,1536]{1,0:T(8,128)} %get-tuple-element.5, s32[32]{0:T(128)S(1)} %add_reduce_fusion, pred[32]{0:T(512)(128)(4,1)S(1)} %and.12), kind=kOutput, calls=%fused_computation.8 | convolution fusion | flops 205948928 | bytes 6947104 | tf_op jit(solution)/shard_map/cm,cw->mw/dot_general | solution.py:70
  100.8 0.8 dynamic-update-slice
  101.5 10.2 %all-reduce = s32[16]{0:T(128)S(1)} all-reduce(s32[16]{0:T(128)S(1)} %dynamic-update-slice), channel_id=1, replica_groups=mesh['grp'=2,'exp'=16] {'exp'}, use_global_device_ids=true, to_apply=%add | all-reduce | flops 16 | bytes 128
  112.3 3.2 %all-to-all-start.3 = ((s32[16,2,1]{0,2,1:T(1,128)}), s32[16,2,1]{0,2,1:T(1,128)S(1)}, u32[]{:S(2)}, u32[]{:S(2)}) async-start(s32[16,2,1]{0,2,1:T(1,128)} %broadcast_in_dim.16), calls=%async_computation.3 | async-start | bytes 2048 | tf_op jit(solution)/shard_map/all_to_all | solution.py:46
  115.5 3.7 %all-to-all-done.3 = s32[16,2,1]{0,2,1:T(1,128)S(1)} async-done(((s32[16,2,1]{0,2,1:T(1,128)}), s32[16,2,1]{0,2,1:T(1,128)S(1)}, u32[]{:S(2)}, u32[]{:S(2)}) %all-to-all-start.3) | async-done | bytes 160 | tf_op jit(solution)/shard_map/all_to_all | solution.py:46
  119.3 68.5 %all-reduce.5.cloned.1.call-done = f32[32,2048]{1,0:T(8,128)} async-done(((f32[32,2048]{1,0:T(8,128)}), f32[32,2048]{1,0:T(8,128)}) %all-reduce.5.cloned.1.call-update) | async-done | bytes 262160 | tf_op jit(solution)/shard_map/psum | solution.py:72
  187.8 1.0 add_convert_fusion
  188.8 6.5 %all_gather.18 = bf16[32,4096]{1,0:T(8,128)(2,1)S(1)} all-gather(bf16[32,2048]{1,0:T(8,128)(2,1)S(1)} %add_convert_fusion), channel_id=1, replica_groups=mesh['grp'=2,'exp'=16] {'grp'}, dimensions={1}, use_global_device_ids=true | all-gather | bytes 393216 | tf_op jit(solution)/shard_map/all_gather | solution.py:75
  195.5 13.7 %exponential_reduce_fusion = (f32[32]{0:T(128)S(1)}, f32[32,4096]{1,0:T(8,128)S(1)}) fusion(f32[32]{0:T(128)S(1)} %add_sqrt_fusion, bf16[4096,4096]{1,0:T(8,128)(2,1)} %param.18, bf16[32,4096]{1,0:T(8,128)(2,1)S(1)} %all_gather.18, f32[4096]{0:T(1024)S(1)} %copy-done.1), kind=kOutput, calls=%fused_computation.17 | convolution fusion | flops 1074528256 | bytes 34357504 | tf_op jit(solution)/shard_map/dot_general | solution.py:77
  209.2 4.9 %psum.52 = f32[32]{0:T(128)S(1)} all-reduce(f32[32]{0:T(128)S(1)} %get-tuple-element.8), channel_id=1, replica_groups=mesh['grp'=2,'exp'=16] {'grp'}, use_global_device_ids=true, to_apply=%region_10.11 | all-reduce | flops 32 | bytes 256 | tf_op jit(solution)/shard_map/psum | solution.py:89
  214.1 29.5 %psum.53 = f32[32]{0:T(128)S(1)} all-reduce(f32[32]{0:T(128)S(1)} %psum.52), channel_id=1, replica_groups=mesh['grp'=2,'exp'=16] {'exp'}, use_global_device_ids=true, to_apply=%region_11.12 | all-reduce | flops 32 | bytes 256 | tf_op jit(solution)/shard_map/psum | solution.py:89
  243.8 4.9 %psum.54 = f32[32]{0:T(128)S(1)} all-reduce(f32[32]{0:T(128)S(1)} %get-tuple-element.2), channel_id=1, replica_groups=mesh['grp'=2,'exp'=16] {'grp'}, use_global_device_ids=true, to_apply=%region_14.15 | all-reduce | flops 32 | bytes 256 | tf_op jit(solution)/shard_map/psum | solution.py:89
  248.7 29.5 %psum.55 = f32[32]{0:T(128)S(1)} all-reduce(f32[32]{0:T(128)S(1)} %psum.54), channel_id=1, replica_groups=mesh['grp'=2,'exp'=16] {'exp'}, use_global_device_ids=true, to_apply=%region_15.16 | all-reduce | flops 32 | bytes 256 | tf_op jit(solution)/shard_map/psum | solution.py:89
  (47 shorter events, 5.8 us)
Async XLA Ops:
  31.2 23.0 %all-to-all-start.1 = ((s32[2,1,128]{2,1,0:T(1,128)}), s32[2,1,128]{2,1,0:T(1,128)S(1)}, u32[]{:S(2)}, u32[]{:S(2)}) async-start(s32[2,1,128]{2,1,0:T(1,128)} %reshape.123), calls=%async_computation.1 | async-start | bytes 2048 | tf_op jit(solution)/shard_map/all_to_all | solution.py:44
  54.2 7.9 %all-to-all-start = ((bf16[16,2,2048]{2,0,1:T(8,128)(2,1)}), bf16[16,2,2048]{2,0,1:T(8,128)(2,1)S(1)}, u32[]{:S(2)}, u32[]{:S(2)}) async-start(bf16[16,2,2048]{2,0,1:T(8,128)(2,1)} %bitcast.52), calls=%async_computation | async-start | bytes 262144 | tf_op jit(solution)/shard_map/all_to_all | solution.py:43
  57.6 36.9 %all-reduce.7.cloned.1.call-start = ((), (), s32[]{:S(2)}) async-start(), calls=%async_computation.5 | async-start | bytes 786432 | tf_op jit(solution)/shard_map/psum | solution.py:65
  62.1 4.9 %copy-start = (bf16[1,2048,1536]{2,1,0:T(8,128)(2,1)S(1)}, bf16[1,2048,1536]{2,1,0:T(8,128)(2,1)}, u32[]{:S(2)}) copy-start(bf16[1,2048,1536]{2,1,0:T(8,128)(2,1)} %param.15) | copy-start | bytes 18874372
  62.3 6.7 %copy-start.3 = (bf16[1,8]{1,0:T(2,128)(2,1)S(1)}, bf16[1,8]{1,0:T(2,128)(2,1)}, u32[]{:S(2)}) copy-start(bf16[1,8]{1,0:T(2,128)(2,1)} %param.12) | copy-start | bytes 52
  67.0 33.1 %copy-start.4 = (u32[32]{0:T(128)S(1)}, u32[32]{0:T(128)}, u32[]{:S(2)}) copy-start(u32[32]{0:T(128)} %constant.59) | copy-start | bytes 388
  67.0 128.4 %copy-start.1 = (f32[4096]{0:T(1024)S(1)}, f32[4096]{0:T(1024)}, u32[]{:S(2)}) copy-start(f32[4096]{0:T(1024)} %param.14) | copy-start | bytes 49156
  68.9 118.9 %all-reduce.5.cloned.1.call-start = ((), (), s32[]{:S(2)}) async-start(), calls=%async_computation.4 | async-start | bytes 524288 | tf_op jit(solution)/shard_map/psum | solution.py:72
  112.3 6.9 %all-to-all-start.3 = ((s32[16,2,1]{0,2,1:T(1,128)}), s32[16,2,1]{0,2,1:T(1,128)S(1)}, u32[]{:S(2)}, u32[]{:S(2)}) async-start(s32[16,2,1]{0,2,1:T(1,128)} %broadcast_in_dim.16), calls=%async_computation.3 | async-start | bytes 2048 | tf_op jit(solution)/shard_map/all_to_all | solution.py:46
  195.5 82.8 %copy-start.2 = (s32[4096]{0:T(1024)S(1)}, s32[4096]{0:T(1024)}, u32[]{:S(2)}) copy-start(s32[4096]{0:T(1024)} %param.19) | copy-start | bytes 49156
Sparse Core Ops, SparseCore 0:
  69.0 23.5 all-reduce.6
  99.6 88.1 all-reduce.4
